TPU v7x, 256 devices: a whole 4x4x8 slice. The times are simulated.
256 devices in a mesh: row: 16 (over z_hi, y, core), col: 16 (over z_lo, x).
Axes of the slice: x: 4, y: 4, z: 8 (z_hi: 2, z_lo: 4; z = z_hi * 4 + z_lo), core: 2. Of those that a mesh axis runs over, the one named last changes fastest.
Arguments:
- features: bfloat16 [65536, 128], P(('col', 'row')), may hold values from -6 to 6
- weight: bfloat16 [128, 128], replicated, may hold values from -0.5 to 0.5
- tiles: bfloat16 [16, 16, 352, 128, 128], P('row', 'col'), may hold values from -0.0546875 to 0.0546875
- tile_slots: int32 [16, 16, 352], P('row', 'col'), may hold values from 0 to 1023, as said below
- tile_counts: int32 [16, 16], P('row', 'col'), may hold values from 44 to 352, as said below
- cotangent: bfloat16 [65536, 128], P(('row', 'col')), may hold values from -6 to 6
Outputs:
- hidden: bfloat16 [65536, 128], P(('row', 'col'))
- feature_grad: bfloat16 [65536, 128], P(('col', 'row'))
- weight_grad: float32 [128, 128], replicated
Inputs may be any that keep to these rules, and one draw needn't show every extreme that they name: `tile_slots`: the slots of one block are distinct. `tile_counts`: some block has all 352 slots live.
All inputs are finite; a program needn't handle non-finite values.
Results may differ from a plain program's by a relative error of at most 0.006.
Values may be sent and summed in bfloat16 or wider, within the bound.
A program may use at most 128 MiB of HBM per device.

v0:
```python
import math

import jax
import jax.numpy as jnp
from jax import lax
from jax.sharding import PartitionSpec as P


def silu_grad(values):
    sig = jax.nn.sigmoid(values)
    return sig * (1.0 + values * (1.0 - sig))


def body(features, weight, tiles, tile_slots, tile_counts, cotangent):
    tile_vals = tiles[0, 0]
    slot_ids = tile_slots[0, 0]
    live_count = tile_counts[0, 0]
    tile_size = tile_vals.shape[-1]
    share_rows = features.shape[0]
    width = features.shape[1]
    slot_total = slot_ids.shape[0]
    row_count = lax.axis_size("row")
    col_count = lax.axis_size("col")
    tile_rows = share_rows * col_count // tile_size
    tile_cols = share_rows * row_count // tile_size
    col_index = lax.axis_index("col")
    projected = jnp.dot(features, weight, preferred_element_type=jnp.float32).astype(jnp.bfloat16)
    proj_block = lax.all_gather(projected, "row", axis=0, tiled=True)
    is_live = jnp.arange(slot_total, dtype=jnp.int32) < live_count
    gathered = proj_block.reshape(tile_cols, tile_size, width)[slot_ids % tile_cols]
    products = jnp.einsum("tij,tjf->tif", tile_vals, gathered, preferred_element_type=jnp.float32)
    fwd_targets = jnp.where(is_live, slot_ids // tile_cols, tile_rows)
    partial_value = jax.ops.segment_sum(products, fwd_targets, tile_rows + 1)[:tile_rows].reshape(
        tile_rows * tile_size, width
    )
    summed = lax.psum(partial_value, "col")
    own_rows = lax.dynamic_slice_in_dim(summed, col_index * share_rows, share_rows, 0)
    hidden = jax.nn.silu(own_rows).astype(jnp.bfloat16)
    cot_block = lax.all_gather(cotangent, "col", axis=0, tiled=True)
    grad_block = (cot_block.astype(jnp.float32) * silu_grad(summed)).astype(jnp.bfloat16)
    grad_tiles = grad_block.reshape(tile_rows, tile_size, width)[slot_ids // tile_cols]
    back_products = jnp.einsum(
        "tji,tjf->tif", tile_vals, grad_tiles, preferred_element_type=jnp.float32
    )
    back_targets = jnp.where(is_live, slot_ids % tile_cols, tile_cols)
    back_partial = jax.ops.segment_sum(back_products, back_targets, tile_cols + 1)[
        :tile_cols
    ].reshape(tile_cols * tile_size, width)
    grad_proj = lax.psum_scatter(back_partial, "row", scatter_dimension=0, tiled=True).astype(
        jnp.bfloat16
    )
    feature_grad = jnp.dot(grad_proj, weight.T, preferred_element_type=jnp.float32).astype(
        jnp.bfloat16
    )
    weight_term = jnp.dot(features.T, grad_proj, preferred_element_type=jnp.float32)
    node_total = share_rows * row_count * col_count
    weight_grad = lax.psum(weight_term, ("row", "col")) / math.sqrt(node_total)
    return (hidden, feature_grad, weight_grad)


def solution(mesh):
    placed = (
        P(("col", "row"), None),
        P(),
        P("row", "col", None, None, None),
        P("row", "col", None),
        P("row", "col"),
        P(("row", "col"), None),
    )
    return jax.shard_map(
        body,
        mesh=mesh,
        in_specs=placed,
        out_specs=(P(("row", "col"), None), P(("col", "row"), None), P()),
        check_vma=False,
    )
```

profile of v0, /device:TPU:24, one launch (start us, length us, event | category | flops | bytes accessed | tf_op | source)
XLA Modules:
  0.0 769.5 jit_solution(9133756063964806921)
XLA Ops:
  7.2 0.0 copy-start
  7.2 0.0 all-gather.3.cloned.1.call-start
  7.2 0.8 copy-done
  8.0 1.5 convolution_convert_fusion.1
  9.5 0.0 all-gather.3.cloned.1.call-update
  9.6 0.0 all-gather.5.cloned.1.call-start
  9.6 0.7 all-gather.5.cloned.1.call-update
  10.3 0.0 all-reduce.3.cloned.1.call-start
  11.0 0.7 fusion.15
  11.7 0.7 fusion.13
  12.4 57.0 %all-gather.3.cloned.1.call-done = bf16[4096,128]{1,0:T(8,128)(2,1)} async-done(((bf16[256,128]{1,0:T(8,128)(2,1)}), bf16[4096,128]{1,0:T(8,128)(2,1)}) %all-gather.3.cloned.1.call-update) | async-done | bytes 1048592 | tf_op jit(solution)/shard_map/all_gather | solution.py:28
  69.4 12.2 %gather_fusion = bf16[352,128,128]{2,1,0:T(8,128)(2,1)} fusion(bf16[32,128,128]{2,1,0:T(8,128)(2,1)} %bitcast.41, s32[1024]{0:T(1024)S(1)} %pad_clamp_fusion.1), kind=kCustom, calls=%fused_computation | custom fusion | bytes 23070080 | tf_op jit(solution)/shard_map/gather | solution.py:30
  81.6 20.6 %fusion.4 = f32[352,128,128]{1,2,0:T(8,128)} fusion(bf16[352,128,128]{2,1,0:T(8,128)(2,1)} %gather_fusion, bf16[1,1,352,128,128]{4,3,2,1,0:T(8,128)(2,1)} %param.8), kind=kOutput, calls=%fused_computation.8 | convolution fusion | flops 1476395008 | bytes 46137344 | tf_op jit(solution)/shard_map/tij,tjf->tif/dot_general | solution.py:31
  102.2 23.5 %copy.13 = f32[352,128,128]{2,1,0:T(8,128)} copy(f32[352,128,128]{1,2,0:T(8,128)} %fusion.4) | data formatting | bytes 46137344 | tf_op jit(solution)/shard_map/tij,tjf->tif/dot_general | solution.py:31
  125.7 0.2 broadcast.191.clone
  125.9 46.0 %scatter_fusion = f32[33,128,128]{2,1,0:T(8,128)S(1)} fusion(f32[33,128,128]{2,1,0:T(8,128)S(1)} %broadcast.191.clone, s32[352]{0:T(512)S(1)} %get-tuple-element.10, f32[352,128,128]{2,1,0:T(8,128)} %copy.13), kind=kCustom, calls=%fused_computation.2 | custom fusion | flops 5767168 | bytes 69207424 | tf_op jit(solution)/shard_map/scatter-add | solution.py:33
  171.9 1.5 slice.12
  173.4 0.0 all-reduce.3.cloned.1.call-update
  173.4 0.2 reduce-scatter.2.cloned.1.call-start
  173.7 0.0 all-gather.5.cloned.1.call-done
  173.7 163.5 %all-reduce.3.cloned.1.call-done = f32[4096,128]{1,0:T(8,128)} async-done(((f32[4096,128]{1,0:T(8,128)}), f32[4096,128]{1,0:T(8,128)}) %all-reduce.3.cloned.1.call-update) | async-done | bytes 2097168 | tf_op jit(solution)/shard_map/psum | solution.py:36
  337.2 2.6 multiply_convert_fusion
  339.9 11.0 %gather_fusion.1 = bf16[352,128,128]{2,1,0:T(8,128)(2,1)} fusion(bf16[32,128,128]{2,1,0:T(8,128)(2,1)S(1)} %bitcast.40, s32[1024]{0:T(1024)S(1)} %pad_clamp_fusion), kind=kCustom, calls=%fused_computation.1 | custom fusion | bytes 23070080 | tf_op jit(solution)/shard_map/gather | solution.py:41
  350.8 14.4 %fusion.7 = f32[352,128,128]{1,2,0:T(8,128)} fusion(bf16[352,128,128]{2,1,0:T(8,128)(2,1)} %gather_fusion.1, bf16[1,1,352,128,128]{4,3,2,1,0:T(8,128)(2,1)} %param.8), kind=kOutput, calls=%fused_computation.9 | convolution fusion | flops 1476395008 | bytes 46137344 | tf_op jit(solution)/shard_map/tji,tjf->tif/dot_general | solution.py:42
  365.3 23.5 %copy.15 = f32[352,128,128]{2,1,0:T(8,128)} copy(f32[352,128,128]{1,2,0:T(8,128)} %fusion.7) | data formatting | bytes 46137344 | tf_op jit(solution)/shard_map/tji,tjf->tif/dot_general | solution.py:42
  388.7 0.2 broadcast.191
  389.0 0.0 copy-start.1
  389.0 46.0 %scatter_fusion.1 = f32[33,128,128]{2,1,0:T(8,128)S(1)} fusion(f32[33,128,128]{2,1,0:T(8,128)S(1)} %broadcast.191, s32[352]{0:T(512)S(1)} %get-tuple-element.11, f32[352,128,128]{2,1,0:T(8,128)} %copy.15), kind=kCustom, calls=%fused_computation.3 | custom fusion | flops 5767168 | bytes 69207424 | tf_op jit(solution)/shard_map/scatter-add | solution.py:46
  435.0 1.5 slice.13
  436.5 0.0 reduce-scatter.2.cloned.1.call-update
  436.5 0.0 all-reduce.5.cloned.1.call-start
  436.6 1.6 multiply_convert_fusion.1
  438.1 84.1 %reduce-scatter.2.cloned.1.call-done = f32[256,128]{1,0:T(8,128)} async-done(((f32[4096,128]{1,0:T(8,128)}), f32[256,128]{1,0:T(8,128)}) %reduce-scatter.2.cloned.1.call-update) | async-done | bytes 131088 | tf_op jit(solution)/shard_map/reduce_scatter | solution.py:49
  522.2 1.7 convolution_bitcast_fusion
  523.9 0.0 all-reduce.5.cloned.1.call-update
  524.0 0.0 copy-done.1
  524.0 1.7 convolution_convert_fusion
  525.7 235.7 %all-reduce.5.cloned.1.call-done = f32[128,128]{0,1:T(8,128)} async-done(((f32[128,128]{0,1:T(8,128)}), f32[128,128]{0,1:T(8,128)}) %all-reduce.5.cloned.1.call-update) | async-done | bytes 65552 | tf_op jit(solution)/shard_map/psum | solution.py:57
  761.4 0.8 broadcast_multiply_fusion
  762.2 0.7 copy.16
  (2 shorter events, 0.0 us)
Async XLA Ops:
  7.2 0.8 copy-start
  7.2 62.2 %all-gather.3.cloned.1.call-start = ((), (), s32[]{:S(2)}) async-start(), calls=%async_computation.1 | async-start | bytes 1114112 | tf_op jit(solution)/shard_map/all_gather | solution.py:28
  9.6 164.1 %all-gather.5.cloned.1.call-start = ((), (), s32[]{:S(2)}) async-start(), calls=%async_computation.3 | async-start | bytes 1114112 | tf_op jit(solution)/shard_map/all_gather | solution.py:39
  10.3 326.9 %all-reduce.3.cloned.1.call-start = ((), (), s32[]{:S(2)}) async-start(), calls=%async_computation.2 | async-start | bytes 4194304 | tf_op jit(solution)/shard_map/psum | solution.py:36
  173.4 348.8 %reduce-scatter.2.cloned.1.call-start = ((), (), s32[]{:S(2)}) async-start(), calls=%async_computation.4 | async-start | bytes 2228224 | tf_op jit(solution)/shard_map/reduce_scatter | solution.py:49
  389.0 135.0 %copy-start.1 = (bf16[128,128]{1,0:T(8,128)(2,1)S(1)}, bf16[128,128]{1,0:T(8,128)(2,1)}, u32[]{:S(2)}) copy-start(bf16[128,128]{1,0:T(8,128)(2,1)} %param.7) | copy-start | bytes 98308
  436.5 324.9 %all-reduce.5.cloned.1.call-start = ((), (), s32[]{:S(2)}) async-start(), calls=%async_computation.5 | async-start | bytes 131072 | tf_op jit(solution)/shard_map/psum | solution.py:57
Sparse Core Ops, SparseCore 0:
  11.3 58.0 all-gather.2
  71.2 77.0 all-gather.4
  173.6 163.6 all-reduce.2
  436.6 85.5 reduce-scatter.1
  528.1 233.1 all-reduce.4
where the time goes:
time: 775 us; the launch traced here: 769 us
  waiting for transfers between devices  541 us (70%)
  other arithmetic  98.5 us (13%)
  local copies, waits for them, and re-layouts  75.1 us (10%)
  matrix products  40 us (5%)
  between operations  14.5 us (2%)
    psum x1, waiting for transfers between devices, body(): weight_grad = lax.psum(weight_term, ('row', 'col')) / math.sqrt(node_total)  236 us
    psum x1, waiting for transfers between devices, body(): summed = lax.psum(partial_value, 'col')  164 us
    reduce_scatter x1, waiting for transfers between devices, body(): lax.psum_scatter(back_partial, 'row', scatter_dimension=0, tiled=True)  84.1 us
    all_gather x1, waiting for transfers between devices, body(): proj_block = lax.all_gather(projected, 'row', axis=0, tiled=True)  57 us
    scatter-add x1, other arithmetic, body(): jax.ops.segment_sum(products, fwd_targets, tile_rows + 1)[:tile_rows]  46 us
    scatter-add x1, other arithmetic, body(): jax.ops.segment_sum(back_products, back_targets, tile_cols + 1)[:tile_cols]  46 us
    dot_general x1, local copies, waits for them, and re-layouts, body(): jnp.einsum('tij,tjf->tif', tile_vals, gathered, preferred_element_type=jn...  23.5 us
    dot_general x1, local copies, waits for them, and re-layouts, body(): jnp.einsum('tji,tjf->tif', tile_vals, grad_tiles, preferred_element_type=...  23.5 us
  transfers between devices with their start and end apart: 5, of which 4 were waited for; matrix products, arithmetic and copies ran while one was open for 14% of the time, Pallas kernels for 0%

commit v1 on v0

v1 whole, which is shorter than its diff:
```python
import functools
import math

import jax
import jax.numpy as jnp
from jax import lax
from jax.experimental import pallas as pl
from jax.experimental.pallas import tpu as pltpu
from jax.sharding import PartitionSpec as P

BF16 = jnp.bfloat16
F32 = jnp.float32

ROW_SPLIT = (2, 4, 2)
COL_SPLIT = (4, 4)


def layer_kernel(dims, smap, feat, wt, tiles, cot, hid, fg, wg, TV, FB, GB, GT, SX, RX, OX, SZ, RZ, SC, RC, SY, RY, OY, SH, RH,
                 W0, W1, WX, WZ, WC, WY, WH, WA, WB, tile_sem, a_send, a_recv, x_send, x_recv, z_send, z_recv, g_send, g_recv,
                 c_send, c_recv, y_send, y_recv, h_send, h_recv, w_send, w_recv):
    ZH, Y, C, ZL, X = dims
    R, Q = ZH * Y * C, ZL * X
    B, F = feat.shape
    T = tiles.shape[-1]
    S = tiles.shape[0]
    U = B // T
    NR, NC = Q * U, R * U
    r, q = lax.axis_index("row"), lax.axis_index("col")
    core, y, zh = r % C, (r // C) % Y, r // (C * Y)
    x, z = q % X, q // X
    rid = lambda h, b, c: (h * Y + b) * C + c
    cid = lambda a, b: a * X + b
    rows_of = lambda blk: pl.ds(pl.multiple_of(blk * B, B), B)
    sends = []

    def put(src, dst, ssem, rsem, **where):
        copy = pltpu.make_async_remote_copy(src_ref=src, dst_ref=dst, send_sem=ssem, recv_sem=rsem, device_id=where,
                                            device_id_type=pl.DeviceIdType.MESH)
        copy.start()
        sends.append(copy)

    def got(dst, ssem, rsem):
        pltpu.make_async_remote_copy(src_ref=dst, dst_ref=dst, send_sem=ssem, recv_sem=rsem, device_id={"row": r},
                                     device_id_type=pl.DeviceIdType.MESH).wait_recv()

    def sent(src, ssem, rsem):
        pltpu.make_async_remote_copy(src_ref=src, dst_ref=src, send_sem=ssem, recv_sem=rsem, device_id={"row": r},
                                     device_id_type=pl.DeviceIdType.MESH).wait_send()

    row_peers = ([rid((zh + d) % ZH, y, core) for d in range(1, ZH)] + [rid(zh, (y + d) % Y, core) for d in range(1, Y)]
                 + [rid(zh, y, (core + d) % C) for d in range(1, C)])
    col_peers = [cid((z + d) % ZL, x) for d in range(1, ZL)] + [cid(z, (x + d) % X) for d in range(1, X)]

    barrier = pltpu.get_barrier_semaphore()
    for p in row_peers:
        pl.semaphore_signal(barrier, inc=1, device_id={"row": p}, device_id_type=pl.DeviceIdType.MESH)
    for p in col_peers:
        pl.semaphore_signal(barrier, inc=1, device_id={"col": p}, device_id_type=pl.DeviceIdType.MESH)
    chunks = tile_sem.shape[0]
    loads = [pltpu.make_async_copy(tiles.at[pl.ds(i * (S // chunks), S // chunks)], TV.at[pl.ds(i * (S // chunks), S // chunks)],
                                   tile_sem.at[i]) for i in range(chunks)]
    for load in loads:
        load.start()
    TV[S] = jnp.zeros((T, T), BF16)
    FB[rows_of(r), :] = feat[...]
    pl.semaphore_wait(barrier, len(row_peers) + len(col_peers))

    n = 0

    def a_put(src, blk, dst_row):
        nonlocal n
        put(src, FB.at[rows_of(blk), :], a_send.at[n], a_recv.at[blk], row=dst_row)
        n += 1

    def a_got(blk):
        got(FB.at[rows_of(blk), :], a_send.at[0], a_recv.at[blk])

    for d in range(1, ZH):
        a_put(feat, r, rid((zh + d) % ZH, y, core))
    for d in range(1, Y):
        a_put(feat, r, rid(zh, (y + d) % Y, core))
    for d in range(1, C):
        a_put(feat, r, rid(zh, y, (core + d) % C))
    for d in range(1, Y):
        blk = rid(zh, (y + d) % Y, core)
        a_got(blk)
        for e in range(1, C):
            a_put(FB.at[rows_of(blk), :], blk, rid(zh, y, (core + e) % C))
    for h in range(1, ZH):
        blk = rid((zh + h) % ZH, y, core)
        a_got(blk)
        for d in range(1, Y):
            a_put(FB.at[rows_of(blk), :], blk, rid(zh, (y + d) % Y, core))
        for e in range(1, C):
            a_put(FB.at[rows_of(blk), :], blk, rid(zh, y, (core + e) % C))
    for h in range(1, ZH):
        for d in range(1, Y):
            blk = rid((zh + h) % ZH, (y + d) % Y, core)
            a_got(blk)
            for e in range(1, C):
                a_put(FB.at[rows_of(blk), :], blk, rid(zh, y, (core + e) % C))
    for e in range(1, C):
        for h in range(ZH):
            for d in range(Y):
                a_got(rid((zh + h) % ZH, (y + d) % Y, (core + e) % C))
    for load in loads:
        load.wait()

    G = 2 if ZL % 2 == 0 else 1

    def forward(xt, zp):
        parts = []
        for k in range(G):
            base = cid(zp * G + k, xt) * (U * NC)
            for u in range(U):
                parts.append(jnp.concatenate([TV[smap[base + (u * NC + c)]] for c in range(NC)], 1))
        return jnp.dot(jnp.concatenate(parts, 0), FB[...], preferred_element_type=F32)

    def far(i, carry):
        d = i // (ZL // G)
        zp = i % (ZL // G)
        xt = (x + 1 + d) % X
        out = forward(xt, zp).astype(BF16)
        for k in range(G):
            zt = zp * G + k
            SX[d, zt] = out[k * B:(k + 1) * B]
            pltpu.make_async_remote_copy(src_ref=SX.at[d, zt], dst_ref=RX.at[d, zt], send_sem=x_send.at[d, zt],
                                         recv_sem=x_recv.at[d, zt], device_id={"col": cid(z, xt)},
                                         device_id_type=pl.DeviceIdType.MESH).start()
        return carry

    def near(zp, carry):
        out = forward(x, zp)
        for k in range(G):
            OX[zp * G + k] = out[k * B:(k + 1) * B]
        return carry

    lax.fori_loop(0, (X - 1) * (ZL // G), far, 0)
    lax.fori_loop(0, ZL // G, near, 0)
    own = None
    for d in list(range(1, ZL)) + [0]:
        zt = (z + d) % ZL
        own = OX[zt]
        for e in range(X - 1):
            got(RX.at[e, zt], x_send.at[e, zt], x_recv.at[e, zt])
            own = own + RX[e, zt].astype(F32)
        if d:
            SZ[d - 1] = own.astype(BF16)
            put(SZ.at[d - 1], RZ.at[d - 1], z_send.at[d - 1], z_recv.at[d - 1], col=cid(zt, x))
    for d in range(1, ZL):
        got(RZ.at[d - 1], z_send.at[d - 1], z_recv.at[d - 1])
        own = own + RZ[d - 1].astype(F32)

    high = own.astype(BF16)
    low = (own - high.astype(F32)).astype(BF16)
    summed = jnp.dot(high, wt[...], preferred_element_type=F32) + jnp.dot(low, wt[...], preferred_element_type=F32)
    sig = jax.nn.sigmoid(summed)
    grad = (cot[...].astype(F32) * (sig * (1.0 + summed * (1.0 - sig)))).astype(BF16)
    GB[rows_of(q), :] = grad

    n_g = 0

    def g_put(blk, dst_col):
        nonlocal n_g
        put(GB.at[rows_of(blk), :], GB.at[rows_of(blk), :], g_send.at[n_g], g_recv.at[blk], col=dst_col)
        n_g += 1

    def g_got(blk):
        got(GB.at[rows_of(blk), :], g_send.at[0], g_recv.at[blk])

    def turn(blk):
        GT[:, rows_of(blk)] = GB[rows_of(blk), :].T

    for d in range(1, ZL):
        g_put(q, cid((z + d) % ZL, x))
    for d in range(1, X):
        g_put(q, cid(z, (x + d) % X))
    hid[...] = (summed * sig).astype(BF16)

    both = (((0,), (0,)), ((), ()))
    W0[...] = lax.dot_general(high, grad, both, preferred_element_type=F32) + lax.dot_general(low, grad, both, preferred_element_type=F32)
    px = F // X
    pz = px // ZL
    n_w = 0

    def w_put(src, dst, at, **where):
        nonlocal n_w
        put(src, dst, w_send.at[n_w], w_recv.at[at], **where)
        n_w += 1

    def w_got(dst, at):
        got(dst, w_send.at[0], w_recv.at[at])

    at_x, at_z = 0, X
    at_c = at_z + ZL
    at_y = at_c + C
    at_h = at_y + Y
    at_a = at_h + ZH
    at_b = at_a + ZL
    part = lambda i, size: pl.ds(pl.multiple_of(i * size, size), size)
    for d in range(1, X):
        xt = (x + d) % X
        w_put(W0.at[part(xt, px), :], WX.at[d], at_x + d, col=cid(z, xt))

    def w_step1():
        total = W0[part(x, px), :]
        for d in range(1, X):
            w_got(WX.at[d], at_x + d)
            total = total + WX[d]
        W1[...] = total
        for d in range(1, ZL):
            zt = (z + d) % ZL
            w_put(W1.at[part(zt, pz), :], WZ.at[d], at_z + d, col=cid(zt, x))

    def w_step2():
        total = W1[part(z, pz), :]
        for d in range(1, ZL):
            w_got(WZ.at[d], at_z + d)
            total = total + WZ[d]
        WC[core] = total
        for d in range(1, C):
            w_put(WC.at[core], WC.at[core], at_c + core, row=rid(zh, y, (core + d) % C))

    def w_step3():
        for d in range(1, C):
            w_got(WC.at[(core + d) % C], at_c + (core + d) % C)
        total = WC[0]
        for i in range(1, C):
            total = total + WC[i]
        WY[y] = total
        for d in range(1, Y):
            w_put(WY.at[y], WY.at[y], at_y + y, row=rid(zh, (y + d) % Y, core))

    def w_step4():
        for d in range(1, Y):
            w_got(WY.at[(y + d) % Y], at_y + (y + d) % Y)
        total = WY[0]
        for i in range(1, Y):
            total = total + WY[i]
        WH[zh] = total
        for d in range(1, ZH):
            w_put(WH.at[zh], WH.at[zh], at_h + zh, row=rid((zh + d) % ZH, y, core))

    def w_step5():
        for d in range(1, ZH):
            w_got(WH.at[(zh + d) % ZH], at_h + (zh + d) % ZH)
        total = WH[0]
        for i in range(1, ZH):
            total = total + WH[i]
        WA[part(z, pz), :] = total
        for d in range(1, ZL):
            w_put(WA.at[part(z, pz), :], WA.at[part(z, pz), :], at_a + z, col=cid((z + d) % ZL, x))

    def w_step6():
        for d in range(1, ZL):
            w_got(WA.at[part((z + d) % ZL, pz), :], at_a + (z + d) % ZL)
        WB[part(x, px), :] = WA[...]
        for d in range(1, X):
            w_put(WA, WB.at[part(x, px), :], at_b + x, col=cid(z, (x + d) % X))

    def w_step7():
        for d in range(1, X):
            w_got(WB.at[part((x + d) % X, px), :], at_b + (x + d) % X)
        wg[...] = WB[...] * (1.0 / math.sqrt(B * R * Q))

    turn(q)
    for d in range(1, ZL):
        blk = cid((z + d) % ZL, x)
        g_got(blk)
        for e in range(1, X):
            g_put(blk, cid(z, (x + e) % X))
        turn(blk)
    w_step1()
    for a in range(ZL):
        for e in range(1, X):
            blk = cid((z + a) % ZL, (x + e) % X)
            g_got(blk)
            turn(blk)
    w_step2()

    def backward(blk):
        base = blk * U
        w = jnp.concatenate([jnp.concatenate([TV[smap[t * NC + base + u]] for u in range(U)], 1) for t in range(NR)], 0)
        return jnp.dot(GT[...], w, preferred_element_type=F32)

    K = ZH * Y

    def other(i, carry):
        d, k = i // K, i % K
        ct = (core + 1 + d) % C
        SC[d, k] = backward(k * C + ct).astype(BF16)
        pltpu.make_async_remote_copy(src_ref=SC.at[d, k], dst_ref=RC.at[d, k], send_sem=c_send.at[d, k], recv_sem=c_recv.at[d, k],
                                     device_id={"row": rid(zh, y, ct)}, device_id_type=pl.DeviceIdType.MESH).start()
        return carry

    def joined(ht, yt):
        k = ht * Y + yt
        out = backward(rid(ht, yt, core))
        for d in range(C - 1):
            got(RC.at[d, k], c_send.at[d, k], c_recv.at[d, k])
            out = out + RC[d, k].astype(F32)
        return out

    def along(i, carry):
        d, ht = i // ZH, i % ZH
        yt = (y + 1 + d) % Y
        SY[d, ht] = joined(ht, yt).astype(BF16)
        pltpu.make_async_remote_copy(src_ref=SY.at[d, ht], dst_ref=RY.at[d, ht], send_sem=y_send.at[d, ht], recv_sem=y_recv.at[d, ht],
                                     device_id={"row": rid(zh, yt, core)}, device_id_type=pl.DeviceIdType.MESH).start()
        return carry

    def stay(i, carry):
        OY[i] = joined((zh + 1 + i) % ZH, y)
        return carry

    half = (C - 1) * K // 2
    lax.fori_loop(0, half, other, 0)
    w_step3()
    lax.fori_loop(half, (C - 1) * K, other, 0)
    w_step4()
    lax.fori_loop(0, (Y - 1) * ZH, along, 0)
    w_step5()
    lax.fori_loop(0, ZH, stay, 0)
    w_step6()
    for i in range(ZH):
        ht = (zh + 1 + i) % ZH
        own = OY[i]
        for d in range(Y - 1):
            got(RY.at[d, ht], y_send.at[d, ht], y_recv.at[d, ht])
            own = own + RY[d, ht].astype(F32)
        if i < ZH - 1:
            SH[i] = own.astype(BF16)
            put(SH.at[i], RH.at[i], h_send.at[i], h_recv.at[i], row=rid(ht, y, core))
    w_step7()
    for i in range(ZH - 1):
        got(RH.at[i], h_send.at[i], h_recv.at[i])
        own = own + RH[i].astype(F32)
    proj = own.astype(BF16).T
    fg[...] = lax.dot_general(proj, wt[...], (((1,), (1,)), ((), ())), preferred_element_type=F32).astype(BF16)

    for copy in sends:
        copy.wait_send()
    for d in range(X - 1):
        for k in range(ZL):
            sent(SX.at[d, k], x_send.at[d, k], x_recv.at[d, k])
    for d in range(C - 1):
        for k in range(K):
            sent(SC.at[d, k], c_send.at[d, k], c_recv.at[d, k])
    for d in range(Y - 1):
        for k in range(ZH):
            sent(SY.at[d, k], y_send.at[d, k], y_recv.at[d, k])


def body(dims, features, weight, tiles, tile_slots, tile_counts, cotangent):
    ZH, Y, C, ZL, X = dims
    R, Q = ZH * Y * C, ZL * X
    tile_vals, slot_ids, live_count = tiles[0, 0], tile_slots[0, 0], tile_counts[0, 0]
    S, T = tile_vals.shape[0], tile_vals.shape[-1]
    B, F = features.shape
    places = (B * Q // T) * (B * R // T)
    order = jnp.arange(S, dtype=jnp.int32)
    hit = (slot_ids[None, :] == jnp.arange(places, dtype=jnp.int32)[:, None]) & (order < live_count)[None, :]
    smap = S + jnp.sum(jnp.where(hit, order - S, 0), axis=1)
    dma = pltpu.SemaphoreType.DMA
    n1 = lambda v: max(v, 1)
    px = F // X
    pz = px // ZL
    blocks = lambda *lead: pltpu.VMEM((*lead, B, F), BF16)
    turned = lambda *lead: pltpu.VMEM((*lead, F, B), BF16)
    n_row = ZH * Y * C - 1
    n_w = 2 * (X - 1) + 2 * (ZL - 1) + (C - 1) + (Y - 1) + (ZH - 1)
    scratch = [
        pltpu.VMEM((S + 1, T, T), BF16),
        pltpu.VMEM((B * R, F), BF16),
        pltpu.VMEM((B * Q, F), BF16),
        pltpu.VMEM((F, B * Q), BF16),
        blocks(n1(X - 1), ZL), blocks(n1(X - 1), ZL),
        pltpu.VMEM((ZL, B, F), F32),
        blocks(n1(ZL - 1)), blocks(n1(ZL - 1)),
        turned(n1(C - 1), ZH * Y), turned(n1(C - 1), ZH * Y),
        turned(n1(Y - 1), ZH), turned(n1(Y - 1), ZH),
        pltpu.VMEM((ZH, F, B), F32),
        turned(n1(ZH - 1)), turned(n1(ZH - 1)),
        pltpu.VMEM((F, F), F32), pltpu.VMEM((px, F), F32),
        pltpu.VMEM((X, px, F), F32), pltpu.VMEM((ZL, pz, F), F32),
        pltpu.VMEM((C, pz, F), F32), pltpu.VMEM((Y, pz, F), F32), pltpu.VMEM((ZH, pz, F), F32),
        pltpu.VMEM((px, F), F32), pltpu.VMEM((F, F), F32),
        dma((8,)),
        dma((n_row,)), dma((R,)),
        dma((n1(X - 1), ZL)), dma((n1(X - 1), ZL)),
        dma((n1(ZL - 1),)), dma((n1(ZL - 1),)),
        dma((Q - 1,)), dma((Q,)),
        dma((n1(C - 1), ZH * Y)), dma((n1(C - 1), ZH * Y)),
        dma((n1(Y - 1), ZH)), dma((n1(Y - 1), ZH)),
        dma((n1(ZH - 1),)), dma((n1(ZH - 1),)),
        dma((n_w,)), dma((2 * X + 2 * ZL + C + Y + ZH,)),
    ]
    vmem = pl.BlockSpec(memory_space=pltpu.VMEM)
    return pl.pallas_call(
        functools.partial(layer_kernel, dims),
        name="graph_layer",
        out_shape=(jax.ShapeDtypeStruct((B, F), BF16), jax.ShapeDtypeStruct((B, F), BF16), jax.ShapeDtypeStruct((F, F), F32)),
        in_specs=[pl.BlockSpec(memory_space=pltpu.SMEM), vmem, vmem, pl.BlockSpec(memory_space=pl.ANY), vmem],
        out_specs=(vmem, vmem, vmem),
        scratch_shapes=scratch,
        compiler_params=pltpu.CompilerParams(collective_id=0, has_side_effects=True, vmem_limit_bytes=60 * 1024 * 1024),
    )(smap, features, weight, tile_vals, cotangent)


def solution(mesh, dims=ROW_SPLIT + COL_SPLIT):
    placed = (
        P(("col", "row"), None),
        P(),
        P("row", "col", None, None, None),
        P("row", "col", None),
        P("row", "col"),
        P(("row", "col"), None),
    )
    return jax.shard_map(
        functools.partial(body, dims),
        mesh=mesh,
        in_specs=placed,
        out_specs=(P(("row", "col"), None), P(("col", "row"), None), P()),
        check_vma=False,
    )
```

time: 775 us -> 89.9 us (0.12)
  waiting for transfers between devices: 541 us -> 0 us
  other arithmetic: 98.5 us -> 1.67 us
  Pallas kernels: 0 us -> 82.2 us
  local copies, waits for them, and re-layouts: 75.1 us -> 4.42 us
  matrix products: 40 us -> 0 us
  between operations: 14.5 us -> 1.31 us
    psum x2 -> x0, waiting for transfers between devices: 399 us -> none  [the longest x1 236 us: body(): weight_grad = lax.psum(weight_term, ('row', 'col')) / math.sqrt(node_total)]
    scatter-add x2 -> x0, other arithmetic: 92 us -> none  [the longest x1 46 us: body(): jax.ops.segment_sum(products, fwd_targets, tile_rows + 1)[:tile_rows]]
    reduce_scatter x1 -> x0, waiting for transfers between devices: 84.1 us -> none  [body(): lax.psum_scatter(back_partial, 'row', scatter_dimension=0, tiled=True)]
    pallas_call x0 -> x1, Pallas kernels: none -> 82.2 us  [body(): pl.pallas_call(functools.partial(layer_kernel, dims), name='graph_layer',...]
    all_gather x2 -> x0, waiting for transfers between devices: 57 us -> none  [the longest x1 57 us: body(): proj_block = lax.all_gather(projected, 'row', axis=0, tiled=True)]
    dot_general x2 -> x0, local copies, waits for them, and re-layouts: 47 us -> none  [the longest x1 23.5 us: body(): jnp.einsum('tij,tjf->tif', tile_vals, gathered, preferred_element_type=jn...]
    dot_general x5 -> x0, matrix products: 40 us -> none  [the longest x1 20.6 us: body(): jnp.einsum('tij,tjf->tif', tile_vals, gathered, preferred_element_type=jn...]
    gather x2 -> x0, local copies, waits for them, and re-layouts: 23.1 us -> none  [the longest x1 12.2 us: body(): proj_block.reshape(tile_cols, tile_size, width)[slot_ids % tile_cols]]
  transfers between devices with their start and end apart: 5 -> 0, of which waited for: 4 -> 0; matrix products, arithmetic and copies ran while one was open for 14% -> 0% of each run, Pallas kernels for 0% -> 0%
where the time goes in v1:
time: 89.9 us; the launch traced here: 89.6 us
  Pallas kernels  82.2 us (91%)
  local copies, waits for them, and re-layouts  4.42 us (5%)
  other arithmetic  1.67 us (2%)
  between operations  1.31 us (1%)
    pallas_call x1, Pallas kernels, body(): pl.pallas_call(functools.partial(layer_kernel, dims), name='graph_layer',...  82.2 us
    unnamed x3, local copies, waits for them, and re-layouts  4.42 us

profile of v1, /device:TPU:24, one launch (start us, length us, event | category | flops | bytes accessed | tf_op | source)
XLA Modules:
  0.0 89.6 jit_solution(12544130769031242319)
XLA Ops:
  1.3 0.7 reduce
  2.0 0.4 select_reduce_fusion
  2.4 0.6 broadcast_add_fusion.smap
  3.0 82.2 %graph_layer.1 = (bf16[256,128]{1,0:T(8,128)(2,1)}, bf16[256,128]{1,0:T(8,128)(2,1)}, f32[128,128]{1,0:T(8,128)}) custom-call(s32[1024]{0:T(1024)} %broadcast_add_fusion.smap, bf16[256,128]{1,0:T(8,128)(2,1)} %feat.1, bf16[128,128]{1,0:T(8,128)(2,1)} %wt.1, bf16[352,128,128]{2,1,0:T(8,128)(2,1)} %bitcast.3, bf16[256,128]{1,0:T(8,128)(2,1)} %cot.1), custom_call_target="tpu_custom_call" | custom-call | tf_op jit(solution)/shard_map/graph_layer/pallas_call | solution.py:399
  85.2 1.5 %copy.13 = bf16[256,128]{1,0:T(8,128)(2,1)} copy(bf16[256,128]{1,0:T(8,128)(2,1)} %get-tuple-element.6) | data formatting | bytes 131072
  86.6 1.5 %copy.14 = bf16[256,128]{1,0:T(8,128)(2,1)} copy(bf16[256,128]{1,0:T(8,128)(2,1)} %get-tuple-element.7) | data formatting | bytes 131072
  88.1 1.5 %copy.15 = f32[128,128]{1,0:T(8,128)} copy(f32[128,128]{1,0:T(8,128)} %get-tuple-element.8) | data formatting | bytes 131072
  (2 shorter events, 0.0 us)

commit v2 on v1

v2 whole, which is shorter than its diff:
```python
import functools
import math

import jax
import jax.numpy as jnp
from jax import lax
from jax.experimental import pallas as pl
from jax.experimental.pallas import tpu as pltpu
from jax.sharding import PartitionSpec as P

BF16 = jnp.bfloat16
F32 = jnp.float32

ROW_SPLIT = (2, 4, 2)
COL_SPLIT = (4, 4)


def layer_kernel(dims, smap, feat, wt, tiles, cot, hid, fg, wg, TV, FB, GB, GT, AX, AR, S2, RP, RM, S1, R1, OX, SZ, RZ, SC, RC,
                 T2, QP, QM, T1, Q1, OY, SH, RH, W0, W1, WX, WZ, WC, WY, WH, WA, WB, tile_sem, a_send, a_recv, p_send, p_recv,
                 m_send, m_recv, x_send, x_recv, z_send, z_recv, g_send, g_recv, c_send, c_recv, u_send, u_recv, v_send, v_recv,
                 y_send, y_recv, h_send, h_recv, w_send, w_recv):
    ZH, Y, C, ZL, X = dims
    R, Q = ZH * Y * C, ZL * X
    B, F = feat.shape
    T = tiles.shape[-1]
    S = tiles.shape[0]
    U = B // T
    NC = R * U
    r, q = lax.axis_index("row"), lax.axis_index("col")
    core, y, zh = r % C, (r // C) % Y, r // (C * Y)
    x, z = q % X, q // X
    rid = lambda h, b, c: (h * Y + b) * C + c
    cid = lambda a, b: a * X + b
    span = lambda i, size: pl.ds(pl.multiple_of(i * size, size), size)
    rows_of = lambda blk: span(blk, B)
    half_of = lambda blk, k: span(blk * 2 + k, B // 2)
    xp, xm, x2 = (x + 1) % X, (x + X - 1) % X, (x + 2) % X
    yp, ym, y2 = (y + 1) % Y, (y + Y - 1) % Y, (y + 2) % Y
    z_near = {1: [], 2: [1 - z], 4: [z + 1 - 2 * (z % 2), (z + 2) % 4, 3 - z]}[ZL]
    h_peers = [(zh + d) % ZH for d in range(1, ZH)]
    c_peers = [(core + d) % C for d in range(1, C)]
    sends = []

    def put(src, dst, ssem, rsem, **where):
        copy = pltpu.make_async_remote_copy(src_ref=src, dst_ref=dst, send_sem=ssem, recv_sem=rsem, device_id=where,
                                            device_id_type=pl.DeviceIdType.MESH)
        copy.start()
        sends.append(copy)

    def got(dst, ssem, rsem):
        pltpu.make_async_remote_copy(src_ref=dst, dst_ref=dst, send_sem=ssem, recv_sem=rsem, device_id={"row": r},
                                     device_id_type=pl.DeviceIdType.MESH).wait_recv()

    row_peers = ([rid(h, y, core) for h in h_peers] + [rid(zh, (y + d) % Y, core) for d in range(1, Y)]
                 + [rid(zh, y, c) for c in c_peers])
    col_peers = [cid(a, x) for a in z_near] + [cid(z, (x + d) % X) for d in range(1, X)]

    barrier = pltpu.get_barrier_semaphore()
    for p in row_peers:
        pl.semaphore_signal(barrier, inc=1, device_id={"row": p}, device_id_type=pl.DeviceIdType.MESH)
    for p in col_peers:
        pl.semaphore_signal(barrier, inc=1, device_id={"col": p}, device_id_type=pl.DeviceIdType.MESH)
    chunks = tile_sem.shape[0]
    loads = [pltpu.make_async_copy(tiles.at[pl.ds(i * (S // chunks), S // chunks)], TV.at[pl.ds(i * (S // chunks), S // chunks)],
                                   tile_sem.at[i]) for i in range(chunks)]
    for load in loads:
        load.start()
    TV[S] = jnp.zeros((T, T), BF16)
    FB[rows_of(r), :] = feat[...]
    pl.semaphore_wait(barrier, len(row_peers) + len(col_peers))

    n_a = 0

    def a_put(at, blk, k, dst_row):
        nonlocal n_a
        put(FB.at[at, :], FB.at[at, :], a_send.at[n_a], a_recv.at[blk, k], row=dst_row)
        n_a += 1

    def a_got(at, blk, k):
        got(FB.at[at, :], a_send.at[0], a_recv.at[blk, k])

    def a_cores(blk):
        for c in c_peers:
            a_put(rows_of(blk), blk, 0, rid(zh, y, c))

    def a_ring(h):
        blk = rid(h, y, core)
        if Y > 1:
            a_put(rows_of(blk), blk, 0, rid(zh, yp, core))
            a_put(rows_of(blk), blk, 0, rid(zh, ym, core))
        a_cores(blk)

    def a_near(h):
        if Y > 1:
            left, right = rid(h, ym, core), rid(h, yp, core)
            a_got(rows_of(left), left, 0)
            a_put(half_of(left, 0), left, 0, rid(zh, yp, core))
            a_cores(left)
            a_got(rows_of(right), right, 0)
            a_put(half_of(right, 1), right, 1, rid(zh, ym, core))
            a_cores(right)

    def a_far(h):
        if Y > 1:
            blk = rid(h, y2, core)
            for k in range(2):
                a_got(half_of(blk, k), blk, k)
            a_cores(blk)

    def a_core(h):
        for c in c_peers:
            for b in range(Y):
                blk = rid(h, (y + b) % Y, c)
                a_got(rows_of(blk), blk, 0)

    for h in h_peers:
        a_put(rows_of(r), r, 0, rid(h, y, core))
    a_ring(zh)
    a_near(zh)
    a_far(zh)
    a_core(zh)
    for load in loads:
        load.wait()

    part_cols = NC // ZH

    def product(cids, h):
        parts = []
        for c in cids:
            for u in range(U):
                base = (c * U + u) * NC + h * part_cols
                parts.append(jnp.concatenate([TV[smap[base + t]] for t in range(part_cols)], 1))
        return jnp.dot(jnp.concatenate(parts, 0), FB[span(h, part_cols * T), :], preferred_element_type=F32)

    G = 2
    hs = [zh] + h_peers
    for at, h in enumerate(hs[:-1]):
        later = hs[at + 1]

        def collect(i, carry, at=at, h=h):
            out = product([i * G + k for k in range(G)], h)
            for k in range(G):
                blk = i * G + k
                AX[blk] = out[k * B:(k + 1) * B] if at == 0 else AX[blk] + out[k * B:(k + 1) * B]
            return carry

        stop = Q // G
        cuts = [0, stop * 3 // 8, stop * 6 // 8, stop]
        lax.fori_loop(cuts[0], cuts[1], collect, 0)
        blk = rid(later, y, core)
        a_got(rows_of(blk), blk, 0)
        a_ring(later)
        lax.fori_loop(cuts[1], cuts[2], collect, 0)
        a_near(later)
        lax.fori_loop(cuts[2], cuts[3], collect, 0)
        a_far(later)
        a_core(later)

    def forward(cids):
        out = product(cids, hs[-1])
        outs = [out[k * B:(k + 1) * B] for k in range(len(cids))]
        return [AX[c] + o for c, o in zip(cids, outs)] if ZH > 1 else outs

    zs = z_near[::-1] + [z]
    H = B // 2
    pairs = [tuple(range(i, min(i + G, ZL))) for i in range(0, ZL, G)]
    if X > 1:
        for pair in pairs:
            for i, out in zip(pair, forward([cid(zs[i], x2) for i in pair])):
                S2[i] = out.astype(BF16)
                put(S2.at[i, pl.ds(0, H)], RP.at[i], p_send.at[i], p_recv.at[i], col=cid(z, xp))
                put(S2.at[i, pl.ds(H, H)], RM.at[i], m_send.at[i], m_recv.at[i], col=cid(z, xm))

    def reduced(i):
        total = OX[i]
        if X > 1:
            for k in range(2):
                got(R1.at[k, i], x_send.at[k, i], x_recv.at[k, i])
                total = total + R1[k, i].astype(F32)
        if i < ZL - 1:
            SZ[i] = total.astype(BF16)
            put(SZ.at[i], RZ.at[i], z_send.at[i], z_recv.at[i], col=cid(zs[i], x))
        return total

    own = None
    for pair in pairs:
        for i, out in zip(pair, forward([cid(zs[i], x) for i in pair])):
            OX[i] = out
        for i in pair:
            if X > 1:
                plus, minus = forward([cid(zs[i], xp), cid(zs[i], xm)])
                got(RP.at[i], p_send.at[i], p_recv.at[i])
                S1[0, i, pl.ds(0, H)] = (plus[:H] + RP[i].astype(F32)).astype(BF16)
                S1[0, i, pl.ds(H, H)] = plus[H:].astype(BF16)
                put(S1.at[0, i], R1.at[0, i], x_send.at[0, i], x_recv.at[0, i], col=cid(z, xp))
                got(RM.at[i], m_send.at[i], m_recv.at[i])
                S1[1, i, pl.ds(0, H)] = minus[:H].astype(BF16)
                S1[1, i, pl.ds(H, H)] = (minus[H:] + RM[i].astype(F32)).astype(BF16)
                put(S1.at[1, i], R1.at[1, i], x_send.at[1, i], x_recv.at[1, i], col=cid(z, xm))
            if i >= 2:
                own = reduced(i - 2)
    for i in range(max(ZL - 2, 0), ZL):
        own = reduced(i)
    for i in range(ZL - 1):
        got(RZ.at[i], z_send.at[i], z_recv.at[i])
        own = own + RZ[i].astype(F32)

    high = own.astype(BF16)
    low = (own - high.astype(F32)).astype(BF16)
    summed = jnp.dot(high, wt[...], preferred_element_type=F32) + jnp.dot(low, wt[...], preferred_element_type=F32)
    sig = jax.nn.sigmoid(summed)
    grad = (cot[...].astype(F32) * (sig * (1.0 + summed * (1.0 - sig)))).astype(BF16)
    GB[rows_of(q), :] = grad

    n_g = 0

    def g_put(at, blk, k, dst_col):
        nonlocal n_g
        put(GB.at[at, :], GB.at[at, :], g_send.at[n_g], g_recv.at[blk, k], col=dst_col)
        n_g += 1

    def g_got(at, blk, k):
        got(GB.at[at, :], g_send.at[0], g_recv.at[blk, k])

    def turn(blk):
        GT[:, rows_of(blk)] = GB[rows_of(blk), :].T

    def g_ring(a):
        if X > 1:
            blk = cid(a, x)
            g_put(rows_of(blk), blk, 0, cid(z, xp))
            g_put(rows_of(blk), blk, 0, cid(z, xm))

    def g_take(a):
        blk = cid(a, x)
        g_got(rows_of(blk), blk, 0)
        g_ring(a)

    def g_near(a):
        turn(cid(a, x))
        if X > 1:
            left, right = cid(a, xm), cid(a, xp)
            g_got(rows_of(left), left, 0)
            g_put(half_of(left, 0), left, 0, cid(z, xp))
            g_got(rows_of(right), right, 0)
            g_put(half_of(right, 1), right, 1, cid(z, xm))
            turn(left)
            turn(right)

    def g_far(a):
        if X > 1:
            blk = cid(a, x2)
            for k in range(2):
                g_got(half_of(blk, k), blk, k)
            turn(blk)

    g_ring(z)
    for a in z_near:
        g_put(rows_of(q), q, 0, cid(a, x))
    hid[...] = (summed * sig).astype(BF16)

    both = (((0,), (0,)), ((), ()))
    W0[...] = lax.dot_general(high, grad, both, preferred_element_type=F32) + lax.dot_general(low, grad, both, preferred_element_type=F32)
    px = F // X
    pz = px // ZL
    n_w = 0

    def w_put(src, dst, at, **where):
        nonlocal n_w
        put(src, dst, w_send.at[n_w], w_recv.at[at], **where)
        n_w += 1

    def w_got(dst, at):
        got(dst, w_send.at[0], w_recv.at[at])

    at_x, at_z = 0, X
    at_c = at_z + ZL
    at_y = at_c + C
    at_h = at_y + Y
    at_a = at_h + ZH
    at_b = at_a + ZL
    for d in range(1, X):
        xt = (x + d) % X
        w_put(W0.at[span(xt, px), :], WX.at[d], at_x + d, col=cid(z, xt))

    def w_step1():
        total = W0[span(x, px), :]
        for d in range(1, X):
            w_got(WX.at[d], at_x + d)
            total = total + WX[d]
        W1[...] = total
        for d in range(1, ZL):
            zt = (z + d) % ZL
            w_put(W1.at[span(zt, pz), :], WZ.at[d], at_z + d, col=cid(zt, x))

    def w_step2():
        total = W1[span(z, pz), :]
        for d in range(1, ZL):
            w_got(WZ.at[d], at_z + d)
            total = total + WZ[d]
        WC[core] = total
        for d in range(1, C):
            w_put(WC.at[core], WC.at[core], at_c + core, row=rid(zh, y, (core + d) % C))

    def w_step3():
        for d in range(1, C):
            w_got(WC.at[(core + d) % C], at_c + (core + d) % C)
        total = WC[0]
        for i in range(1, C):
            total = total + WC[i]
        WY[y] = total
        for d in range(1, Y):
            w_put(WY.at[y], WY.at[y], at_y + y, row=rid(zh, (y + d) % Y, core))

    def w_step4():
        for d in range(1, Y):
            w_got(WY.at[(y + d) % Y], at_y + (y + d) % Y)
        total = WY[0]
        for i in range(1, Y):
            total = total + WY[i]
        WH[zh] = total
        for d in range(1, ZH):
            w_put(WH.at[zh], WH.at[zh], at_h + zh, row=rid((zh + d) % ZH, y, core))

    def w_step5():
        for d in range(1, ZH):
            w_got(WH.at[(zh + d) % ZH], at_h + (zh + d) % ZH)
        total = WH[0]
        for i in range(1, ZH):
            total = total + WH[i]
        WA[span(z, pz), :] = total
        for d in range(1, ZL):
            w_put(WA.at[span(z, pz), :], WA.at[span(z, pz), :], at_a + z, col=cid((z + d) % ZL, x))

    def w_step6():
        for d in range(1, ZL):
            w_got(WA.at[span((z + d) % ZL, pz), :], at_a + (z + d) % ZL)
        WB[span(x, px), :] = WA[...]
        for d in range(1, X):
            w_put(WA, WB.at[span(x, px), :], at_b + x, col=cid(z, (x + d) % X))

    def w_step7():
        for d in range(1, X):
            w_got(WB.at[span((x + d) % X, px), :], at_b + (x + d) % X)
        wg[...] = WB[...] * (1.0 / math.sqrt(B * R * Q))

    chunk = X * U

    def back(blk, a):
        w = jnp.concatenate([jnp.concatenate([TV[smap[(a * chunk + t) * NC + blk * U + u]] for u in range(U)], 1)
                             for t in range(chunk)], 0)
        return jnp.dot(GT[:, span(a, chunk * T)], w, preferred_element_type=F32)

    order = [z] + z_near

    def gather_back(at, lo, hi):
        def step(blk, carry):
            out = back(blk, order[at])
            AR[blk] = out if at == 0 else AR[blk] + out
            return carry

        lax.fori_loop(lo, hi, step, 0)

    for a in z_near[:1]:
        g_take(a)
    g_near(z)
    w_step1()
    for a in z_near[1:]:
        g_take(a)
    later = [w_step2, w_step3, w_step4]
    if ZL > 1:
        g_near(order[1])
    g_far(z)
    for at in range(ZL - 1):
        gather_back(at, 0, R // 2)
        if at + 2 < ZL:
            g_near(order[at + 2])
        if later:
            later.pop(0)()
        gather_back(at, R // 2, R)
        g_far(order[at + 1])
    for step in later:
        step()

    def last(blk):
        out = back(blk, order[-1])
        return AR[blk] + out if ZL > 1 else out

    E = F // 2
    places = [(i, j, h, b) for i, h in enumerate(h_peers + [zh]) for j, b in enumerate([y2, yp, ym, y] if Y > 1 else [y])]
    for d, c in enumerate(c_peers):
        for k, (i, j, h, b) in enumerate(places):
            SC[d, k] = last(rid(h, b, c)).astype(BF16)
            put(SC.at[d, k], RC.at[d, k], c_send.at[d, k], c_recv.at[d, k], row=rid(zh, y, c))
    w_step5()

    def settled(i):
        total = OY[i]
        if Y > 1:
            for k in range(2):
                got(Q1.at[k, i], y_send.at[k, i], y_recv.at[k, i])
                total = total + Q1[k, i].astype(F32)
        if i < ZH - 1:
            SH[i] = total.astype(BF16)
            put(SH.at[i], RH.at[i], h_send.at[i], h_recv.at[i], row=rid(h_peers[i], y, core))
        return total

    for k, (i, j, h, b) in enumerate(places):
        out = last(rid(h, b, core))
        for d in range(C - 1):
            got(RC.at[d, k], c_send.at[d, k], c_recv.at[d, k])
            out = out + RC[d, k].astype(F32)
        if Y == 1 or j == 3:
            OY[i] = out
        elif j == 0:
            T2[i] = out.astype(BF16)
            put(T2.at[i, pl.ds(0, E)], QP.at[i], u_send.at[i], u_recv.at[i], row=rid(zh, yp, core))
            put(T2.at[i, pl.ds(E, E)], QM.at[i], v_send.at[i], v_recv.at[i], row=rid(zh, ym, core))
        elif j == 1:
            got(QP.at[i], u_send.at[i], u_recv.at[i])
            T1[0, i, pl.ds(0, E)] = (out[:E] + QP[i].astype(F32)).astype(BF16)
            T1[0, i, pl.ds(E, E)] = out[E:].astype(BF16)
            put(T1.at[0, i], Q1.at[0, i], y_send.at[0, i], y_recv.at[0, i], row=rid(zh, yp, core))
        else:
            got(QM.at[i], v_send.at[i], v_recv.at[i])
            T1[1, i, pl.ds(0, E)] = out[:E].astype(BF16)
            T1[1, i, pl.ds(E, E)] = (out[E:] + QM[i].astype(F32)).astype(BF16)
            put(T1.at[1, i], Q1.at[1, i], y_send.at[1, i], y_recv.at[1, i], row=rid(zh, ym, core))
    own = settled(0)
    w_step6()
    for i in range(1, ZH):
        own = settled(i)
    w_step7()
    for i in range(ZH - 1):
        got(RH.at[i], h_send.at[i], h_recv.at[i])
        own = own + RH[i].astype(F32)
    proj = own.astype(BF16).T
    fg[...] = lax.dot_general(proj, wt[...], (((1,), (1,)), ((), ())), preferred_element_type=F32).astype(BF16)

    for copy in sends:
        copy.wait_send()


def place_kernel(a, b, c, oa, ob, oc):
    oa[...] = a[...]
    ob[...] = b[...]
    oc[...] = c[...]


def body(dims, features, weight, tiles, tile_slots, tile_counts, cotangent):
    ZH, Y, C, ZL, X = dims
    R, Q = ZH * Y * C, ZL * X
    tile_vals, slot_ids, live_count = tiles[0, 0], tile_slots[0, 0], tile_counts[0, 0]
    S, T = tile_vals.shape[0], tile_vals.shape[-1]
    B, F = features.shape
    places = (B * Q // T) * (B * R // T)
    order = jnp.arange(S, dtype=jnp.int32)
    hit = (slot_ids[None, :] == jnp.arange(places, dtype=jnp.int32)[:, None]) & (order < live_count)[None, :]
    smap = S + jnp.sum(jnp.where(hit, order - S, 0), axis=1)
    dma = pltpu.SemaphoreType.DMA
    n1 = lambda v: max(v, 1)
    px = F // X
    pz = px // ZL
    blocks = lambda *lead: pltpu.VMEM((*lead, B, F), BF16)
    turned = lambda *lead: pltpu.VMEM((*lead, F, B), BF16)
    half = lambda n: pltpu.VMEM((n, B // 2, F), BF16)
    thin = lambda n: pltpu.VMEM((n, F // 2, B), BF16)
    n_a = R * 2 + 8
    n_g = Q * 2 + 8
    n_w = 2 * (X - 1) + 2 * (ZL - 1) + (C - 1) + (Y - 1) + (ZH - 1)
    scratch = [
        pltpu.VMEM((S + 1, T, T), BF16),
        pltpu.VMEM((B * R, F), BF16),
        pltpu.VMEM((B * Q, F), BF16),
        pltpu.VMEM((F, B * Q), BF16),
        pltpu.VMEM((Q, B, F), F32), pltpu.VMEM((R, F, B), F32),
        blocks(ZL), half(ZL), half(ZL),
        blocks(2, ZL), blocks(2, ZL),
        pltpu.VMEM((ZL, B, F), F32),
        blocks(n1(ZL - 1)), blocks(n1(ZL - 1)),
        turned(n1(C - 1), ZH * Y), turned(n1(C - 1), ZH * Y),
        turned(ZH), thin(ZH), thin(ZH),
        turned(2, ZH), turned(2, ZH),
        pltpu.VMEM((ZH, F, B), F32),
        turned(n1(ZH - 1)), turned(n1(ZH - 1)),
        pltpu.VMEM((F, F), F32), pltpu.VMEM((px, F), F32),
        pltpu.VMEM((X, px, F), F32), pltpu.VMEM((ZL, pz, F), F32),
        pltpu.VMEM((C, pz, F), F32), pltpu.VMEM((Y, pz, F), F32), pltpu.VMEM((ZH, pz, F), F32),
        pltpu.VMEM((px, F), F32), pltpu.VMEM((F, F), F32),
        dma((8,)),
        dma((n_a,)), dma((R, 2)),
        dma((ZL,)), dma((ZL,)), dma((ZL,)), dma((ZL,)),
        dma((2, ZL)), dma((2, ZL)),
        dma((n1(ZL - 1),)), dma((n1(ZL - 1),)),
        dma((n_g,)), dma((Q, 2)),
        dma((n1(C - 1), ZH * Y)), dma((n1(C - 1), ZH * Y)),
        dma((ZH,)), dma((ZH,)), dma((ZH,)), dma((ZH,)),
        dma((2, ZH)), dma((2, ZH)),
        dma((n1(ZH - 1),)), dma((n1(ZH - 1),)),
        dma((n_w,)), dma((2 * X + 2 * ZL + C + Y + ZH,)),
    ]
    vmem = pl.BlockSpec(memory_space=pltpu.VMEM)
    outs = (jax.ShapeDtypeStruct((B, F), BF16), jax.ShapeDtypeStruct((B, F), BF16), jax.ShapeDtypeStruct((F, F), F32))
    found = pl.pallas_call(
        functools.partial(layer_kernel, dims),
        name="graph_layer",
        out_shape=outs,
        in_specs=[pl.BlockSpec(memory_space=pltpu.SMEM), vmem, vmem, pl.BlockSpec(memory_space=pl.ANY), vmem],
        out_specs=(vmem, vmem, vmem),
        scratch_shapes=scratch,
        compiler_params=pltpu.CompilerParams(collective_id=0, has_side_effects=True, vmem_limit_bytes=60 * 1024 * 1024),
    )(smap, features, weight, tile_vals, cotangent)
    return pl.pallas_call(place_kernel, name="place_outputs", out_shape=outs, in_specs=[vmem] * 3, out_specs=(vmem,) * 3)(*found)


def solution(mesh, dims=ROW_SPLIT + COL_SPLIT):
    placed = (
        P(("col", "row"), None),
        P(),
        P("row", "col", None, None, None),
        P("row", "col", None),
        P("row", "col"),
        P(("row", "col"), None),
    )
    return jax.shard_map(
        functools.partial(body, dims),
        mesh=mesh,
        in_specs=placed,
        out_specs=(P(("row", "col"), None), P(("col", "row"), None), P()),
        check_vma=False,
    )
```

time: 89.9 us -> 89.2 us (level); the launches traced: 89.6 us -> 87.8 us
  local copies, waits for them, and re-layouts: 4.42 us -> 0 us
  Pallas kernels: 82.2 us -> 84.8 us
    unnamed x3 -> x0, local copies, waits for them, and re-layouts: 4.42 us -> none
    pallas_call x0 -> x1, Pallas kernels: none -> 1.58 us  [body(): pl.pallas_call(place_kernel, name='place_outputs', out_shape=outs, in_spe...]
    pallas_call x1, Pallas kernels: 82.2 us -> 83.2 us  [body(): pl.pallas_call(functools.partial(layer_kernel, dims), name='graph_layer',...]
where the time goes in v2:
time: 89.2 us; the launch traced here: 87.8 us
  Pallas kernels  84.8 us (95%)
  other arithmetic  1.67 us (2%)
  between operations  1.31 us (1%)
    pallas_call x1, Pallas kernels, body(): pl.pallas_call(functools.partial(layer_kernel, dims), name='graph_layer',...  83.2 us

profile of v2, /device:TPU:24, one launch (start us, length us, event | category | flops | bytes accessed | tf_op | source)
XLA Modules:
  0.0 87.8 jit_solution(57328149865655818)
XLA Ops:
  1.3 0.7 reduce
  2.0 0.4 select_reduce_fusion
  2.4 0.6 broadcast_add_fusion.smap
  3.0 83.2 %graph_layer.1 = (bf16[256,128]{1,0:T(8,128)(2,1)}, bf16[256,128]{1,0:T(8,128)(2,1)}, f32[128,128]{1,0:T(8,128)}) custom-call(s32[1024]{0:T(1024)} %broadcast_add_fusion.smap, bf16[256,128]{1,0:T(8,128)(2,1)} %feat.1, bf16[128,128]{1,0:T(8,128)(2,1)} %wt.1, bf16[352,128,128]{2,1,0:T(8,128)(2,1)} %bitcast.3, bf16[256,128]{1,0:T(8,128)(2,1)} %cot.1), custom_call_target="tpu_custom_call" | custom-call | tf_op jit(solution)/shard_map/graph_layer/pallas_call | solution.py:504
  86.2 1.6 %place_outputs.1 = (bf16[256,128]{1,0:T(8,128)(2,1)}, bf16[256,128]{1,0:T(8,128)(2,1)}, f32[128,128]{1,0:T(8,128)}) custom-call(bf16[256,128]{1,0:T(8,128)(2,1)} %get-tuple-element.6.a, bf16[256,128]{1,0:T(8,128)(2,1)} %get-tuple-element.7.b, f32[128,128]{1,0:T(8,128)} %get-tuple-element.8.c), custom_call_target="tpu_custom_call" | custom-call | tf_op jit(solution)/shard_map/place_outputs/pallas_call | solution.py:513
  (2 shorter events, 0.0 us)
